TPU v7x, 512 devices: a whole 4x8x8 slice. The times are simulated.
512 devices in a mesh: items: 8 (over y), codes: 64 (over x, z, core).
Axes of the slice: x: 4, y: 8, z: 8, core: 2. Of those that a mesh axis runs over, the one named last changes fastest.
Arguments:
- residuals: bfloat16 [8192, 256], P(('items', 'codes')), may hold values from -6 to 6
- codebook: bfloat16 [16384, 256], P('codes'), may hold values from -6 to 6
Outputs:
- new_codebook: float32 [16384, 256], P('codes')
- next_residuals: float32 [8192, 256], P(('items', 'codes'))
All inputs are finite; a program needn't handle non-finite values.
Results may differ from a plain program's by a relative error of at most 0.0024.
Values may be sent and summed in bfloat16 or wider, within the bound.
No kernel may reach another device: no remote copies, remote signals or barrier semaphores. Data moves between devices by JAX's collectives and lax.ppermute only.
A program may use at most 64 MiB of HBM per device.

v0:
```python
import jax
import jax.numpy as jnp
from jax import lax
from jax.sharding import PartitionSpec as P

ITERS = 3
EPSILON = 1e-06
SHARPNESS = 40.0


def shards(residuals, codebook):
    gathered = lax.all_gather(residuals, "codes", axis=0, tiled=True)
    feature_count = gathered.shape[1]
    rows_float = gathered.astype(jnp.float32)
    codes_float = codebook.astype(jnp.float32)
    row_scale = lax.rsqrt(jnp.mean(rows_float * rows_float, axis=1) + EPSILON)
    code_scale = lax.rsqrt(jnp.mean(codes_float * codes_float, axis=1) + EPSILON)
    similarity = lax.dot_general(
        gathered, codebook, (((1,), (1,)), ((), ())), preferred_element_type=jnp.float32
    )
    kernel = jnp.exp(
        SHARPNESS * similarity * row_scale[:, None] * code_scale[None, :] / feature_count
    )
    balance = gathered.shape[0] * lax.axis_size("items") / codebook.shape[0]
    weights_rows = jnp.ones((gathered.shape[0],), jnp.float32)
    weights_cols = jnp.ones((codebook.shape[0],), jnp.float32)
    for sweep in range(ITERS):
        column_total = lax.psum(
            jnp.dot(weights_rows, kernel, precision=lax.Precision.HIGHEST), "items"
        )
        weights_cols = balance / column_total
        row_total = lax.psum(
            jnp.dot(kernel, weights_cols, precision=lax.Precision.HIGHEST), "codes"
        )
        weights_rows = 1.0 / row_total
    transport = (kernel * weights_rows[:, None] * weights_cols[None, :]).astype(jnp.bfloat16)
    numerator = lax.dot_general(
        transport, gathered, (((0,), (0,)), ((), ())), preferred_element_type=jnp.float32
    )
    mass = jnp.sum(transport.astype(jnp.float32), axis=0)
    numerator, mass = lax.psum((numerator, mass), "items")
    new_codebook = numerator / mass[:, None]
    moved = lax.all_to_all(transport, "codes", split_axis=0, concat_axis=1, tiled=True)
    rebuilt = jnp.dot(
        moved,
        lax.all_gather(codebook, "codes", axis=0, tiled=True),
        preferred_element_type=jnp.float32,
    )
    following = residuals.astype(jnp.float32) - rebuilt
    return (new_codebook, following)


def solution(mesh):
    return jax.shard_map(
        shards,
        mesh=mesh,
        in_specs=(P(("items", "codes"), None), P("codes", None)),
        out_specs=(P("codes", None), P(("items", "codes"), None)),
        check_vma=False,
    )
```

profile of v0, /device:TPU:1, one launch (start us, length us, event | category | flops | bytes accessed | tf_op | source)
XLA Modules:
  0.0 592.9 jit_solution(12532103684570617176)
XLA Ops:
  8.0 0.0 copy-start
  8.0 0.0 all-reduce.2.cloned.1.call-start
  8.1 57.9 %all_gather.6 = bf16[1024,256]{1,0:T(8,128)(2,1)S(1)} all-gather(bf16[16,256]{1,0:T(8,128)(2,1)} %param.2), channel_id=1, replica_groups=mesh['items'=8,'codes'=64] {'codes'}, dimensions={0}, use_global_device_ids=true | all-gather | bytes 532480 | tf_op jit(solution)/shard_map/all_gather | solution.py:12
  65.9 1.0 multiply_reduce_fusion.1
  67.0 0.2 multiply_reduce_fusion
  67.2 1.3 fusion.2
  68.5 0.5 fusion.3
  69.0 13.9 %psum.56 = f32[256]{0:T(256)S(1)} all-reduce(f32[256]{0:T(256)S(1)} %bitcast.44), channel_id=1, replica_groups=mesh['items'=8,'codes'=64] {'items'}, use_global_device_ids=true, to_apply=%region_2.0 | all-reduce | flops 256 | bytes 2048 | tf_op jit(solution)/shard_map/psum | solution.py:28
  82.9 1.0 fusion.6
  83.9 127.3 %psum.57 = f32[1024]{0:T(1024)S(1)} all-reduce(f32[1024]{0:T(1024)S(1)} %bitcast.34), channel_id=1, replica_groups=mesh['items'=8,'codes'=64] {'codes'}, use_global_device_ids=true, to_apply=%region_3.0 | all-reduce | flops 1024 | bytes 8192 | tf_op jit(solution)/shard_map/psum | solution.py:32
  211.2 0.5 fusion.7
  211.7 11.2 %psum.58 = f32[256]{0:T(256)S(1)} all-reduce(f32[256]{0:T(256)S(1)} %bitcast.41), channel_id=1, replica_groups=mesh['items'=8,'codes'=64] {'items'}, use_global_device_ids=true, to_apply=%region_4.0 | all-reduce | flops 256 | bytes 2048 | tf_op jit(solution)/shard_map/psum | solution.py:28
  222.9 1.0 fusion.8
  223.9 127.8 %psum.59 = f32[1024]{0:T(1024)S(1)} all-reduce(f32[1024]{0:T(1024)S(1)} %bitcast.36), channel_id=1, replica_groups=mesh['items'=8,'codes'=64] {'codes'}, use_global_device_ids=true, to_apply=%region_5.0 | all-reduce | flops 1024 | bytes 8192 | tf_op jit(solution)/shard_map/psum | solution.py:32
  351.7 0.5 fusion.9
  352.2 11.6 %psum.60 = f32[256]{0:T(256)S(1)} all-reduce(f32[256]{0:T(256)S(1)} %bitcast.43), channel_id=1, replica_groups=mesh['items'=8,'codes'=64] {'items'}, use_global_device_ids=true, to_apply=%region_6.0 | all-reduce | flops 256 | bytes 2048 | tf_op jit(solution)/shard_map/psum | solution.py:28
  363.8 1.0 fusion.10
  364.8 127.8 %psum.61 = f32[1024]{0:T(1024)S(1)} all-reduce(f32[1024]{0:T(1024)S(1)} %bitcast.38), channel_id=1, replica_groups=mesh['items'=8,'codes'=64] {'codes'}, use_global_device_ids=true, to_apply=%region_7.0 | all-reduce | flops 1024 | bytes 8192 | tf_op jit(solution)/shard_map/psum | solution.py:32
  492.6 1.1 convert_reduce_fusion
  493.7 2.1 fusion.11
  495.8 0.0 all-reduce.2.cloned.1.call-update
  495.8 0.0 all-gather.2.cloned.1.call-start
  495.8 0.5 all-gather.2.cloned.1.call-update
  496.4 4.7 all-to-all-start
  501.1 12.6 %psum.63 = f32[256]{0:T(256)S(1)} all-reduce(f32[256]{0:T(256)S(1)} %get-tuple-element.2), channel_id=1, replica_groups=mesh['items'=8,'codes'=64] {'items'}, use_global_device_ids=true, to_apply=%region_10.0 | all-reduce | flops 256 | bytes 2048 | tf_op jit(solution)/shard_map/psum | solution.py:41
  513.7 46.6 %all-reduce.2.cloned.1.call-done = f32[256,256]{1,0:T(8,128)} async-done(((f32[256,256]{1,0:T(8,128)}), f32[256,256]{1,0:T(8,128)}) %all-reduce.2.cloned.1.call-update) | async-done | bytes 262160 | tf_op jit(solution)/shard_map/psum | solution.py:41
  560.3 1.8 broadcast_divide_fusion
  562.1 0.0 all-to-all-done
  562.1 18.1 %all-gather.2.cloned.1.call-done = bf16[16384,256]{1,0:T(8,128)(2,1)} async-done(((bf16[256,256]{1,0:T(8,128)(2,1)}), bf16[16384,256]{1,0:T(8,128)(2,1)}) %all-gather.2.cloned.1.call-update) | async-done | bytes 8388624 | tf_op jit(solution)/shard_map/all_gather | solution.py:46
  580.2 0.0 copy-done
  580.2 5.2 convolution_subtract_fusion
  (9 shorter events, 0.1 us)
Async XLA Ops:
  8.0 572.3 %copy-start = (bf16[16,256]{1,0:T(8,128)(2,1)S(1)}, bf16[16,256]{1,0:T(8,128)(2,1)}, u32[]{:S(2)}) copy-start(bf16[16,256]{1,0:T(8,128)(2,1)} %param.2) | copy-start | bytes 24580
  8.0 552.3 %all-reduce.2.cloned.1.call-start = ((), (), s32[]{:S(2)}) async-start(), calls=%async_computation.1 | async-start | bytes 524288 | tf_op jit(solution)/shard_map/psum | solution.py:41
  495.8 84.5 %all-gather.2.cloned.1.call-start = ((), (), s32[]{:S(2)}) async-start(), calls=%async_computation.2 | async-start | bytes 8519680 | tf_op jit(solution)/shard_map/all_gather | solution.py:46
  496.4 65.7 %all-to-all-start = ((bf16[64,16,256]{2,1,0:T(8,128)(2,1)}), bf16[64,16,256]{2,1,0:T(8,128)(2,1)S(1)}, u32[]{:S(2)}, u32[]{:S(2)}) async-start(bf16[64,16,256]{2,1,0:T(8,128)(2,1)} %bitcast.11), calls=%async_computation | async-start | bytes 1048576 | tf_op jit(solution)/shard_map/all_to_all | solution.py:43
Sparse Core Ops, SparseCore 0:
  495.9 64.3 all-reduce.1
Sparse Core Ops, SparseCore 1:
  499.6 80.5 all-gather.1
where the time goes:
time: 593 us
  blocking collectives  490 us (83%)
  waiting for transfers between devices  65.2 us (11%)
  between operations  15.5 us (3%)
  matrix products  13 us (2%)
    psum x3, blocking collectives, shards(): lax.psum(jnp.dot(kernel, weights_cols, precision=lax.Precision.HIGHEST),...  383 us
    all_gather x1, blocking collectives, shards(): gathered = lax.all_gather(residuals, 'codes', axis=0, tiled=True)  57.9 us
    psum x1, waiting for transfers between devices, shards(): numerator, mass = lax.psum((numerator, mass), 'items')  46.6 us
    psum x3, blocking collectives, shards(): lax.psum(jnp.dot(weights_rows, kernel, precision=lax.Precision.HIGHEST),...  36.7 us
    all_gather x1, waiting for transfers between devices, shards(): lax.all_gather(codebook, 'codes', axis=0, tiled=True)  18.1 us
    psum x1, blocking collectives, shards(): numerator, mass = lax.psum((numerator, mass), 'items')  12.6 us
  transfers between devices with their start and end apart: 3, of which 2 were waited for; matrix products, arithmetic and copies ran while one was open for 0% of the time, Pallas kernels for 0%

commit v1 on v0

--- a/solution.py
+++ b/solution.py
@@ -1,3 +1,4 @@
+import functools
 import jax
 import jax.numpy as jnp
 from jax import lax
@@ -8,8 +9,24 @@
 SHARPNESS = 40.0
 
 
+def point_the_layers_all(t0, device_axis):
+    oldest = jnp.concatenate(
+        lax.all_to_all(
+            jnp.stack([t0] * lax.axis_size(device_axis), axis=0),
+            axis_name=device_axis,
+            split_axis=0,
+            concat_axis=0,
+        ),
+        axis=0,
+    )
+    return oldest
+
+
+divide_the_frames = functools.partial(point_the_layers_all, device_axis="codes")
+
+
 def shards(residuals, codebook):
-    gathered = lax.all_gather(residuals, "codes", axis=0, tiled=True)
+    gathered = divide_the_frames(residuals)
     feature_count = gathered.shape[1]
     rows_float = gathered.astype(jnp.float32)
     codes_float = codebook.astype(jnp.float32)

time: 593 us -> 569 us (0.960)
  blocking collectives: 490 us -> 432 us
  waiting for transfers between devices: 65.2 us -> 81.6 us
  starting transfers between devices: 4.8 us -> 19.6 us
    all_gather x1 -> x0, blocking collectives: 57.9 us -> none  [shards(): gathered = lax.all_gather(residuals, 'codes', axis=0, tiled=True)]
    all_to_all x0 -> x1, waiting for transfers between devices: none -> 16.2 us  [point_the_layers_all(): lax.all_to_all(jnp.stack([t0] * lax.axis_size(device_axis), axis=0), axis...]
    all_to_all x0 -> x1, starting transfers between devices: none -> 14.8 us  [point_the_layers_all(): lax.all_to_all(jnp.stack([t0] * lax.axis_size(device_axis), axis=0), axis...]
  transfers between devices with their start and end apart: 3 -> 4, of which waited for: 2 -> 3; matrix products, arithmetic and copies ran while one was open for 0% -> 0% of each run, Pallas kernels for 0% -> 0%
where the time goes in v1:
time: 569 us; the launch traced here: 568 us
  blocking collectives  432 us (76%)
  waiting for transfers between devices  81.6 us (14%)
  starting transfers between devices  19.6 us (3%)
  between operations  15.5 us (3%)
  matrix products  13 us (2%)
    psum x3, blocking collectives, shards(): lax.psum(jnp.dot(kernel, weights_cols, precision=lax.Precision.HIGHEST),...  383 us
    psum x1, waiting for transfers between devices, shards(): numerator, mass = lax.psum((numerator, mass), 'items')  46.5 us
    psum x3, blocking collectives, shards(): lax.psum(jnp.dot(weights_rows, kernel, precision=lax.Precision.HIGHEST),...  36.7 us
    all_gather x1, waiting for transfers between devices, shards(): lax.all_gather(codebook, 'codes', axis=0, tiled=True)  18.4 us
    all_to_all x1, waiting for transfers between devices, point_the_layers_all(): lax.all_to_all(jnp.stack([t0] * lax.axis_size(device_axis), axis=0), axis...  16.2 us
    all_to_all x1, starting transfers between devices, point_the_layers_all(): lax.all_to_all(jnp.stack([t0] * lax.axis_size(device_axis), axis=0), axis...  14.8 us
    psum x1, blocking collectives, shards(): numerator, mass = lax.psum((numerator, mass), 'items')  12.6 us
  transfers between devices with their start and end apart: 4, of which 3 were waited for; matrix products, arithmetic and copies ran while one was open for 0% of the time, Pallas kernels for 0%

profile of v1, /device:TPU:1, one launch (start us, length us, event | category | flops | bytes accessed | tf_op | source)
XLA Modules:
  0.0 567.9 jit_solution(10860303087291857490)
XLA Ops:
  8.0 0.0 copy-start
  8.0 1.6 stack.2
  9.6 14.8 %all-to-all-start = ((bf16[64,16,256]{2,1,0:T(8,128)(2,1)}), bf16[64,16,256]{2,1,0:T(8,128)(2,1)S(1)}, u32[]{:S(2)}, u32[]{:S(2)}) async-start(bf16[64,16,256]{2,1,0:T(8,128)(2,1)} %stack.2), calls=%async_computation | async-start | bytes 1048576 | tf_op jit(solution)/shard_map/all_to_all | solution.py:14
  24.4 0.0 all-reduce.2.cloned.1.call-start
  24.5 1.0 multiply_reduce_fusion.1
  25.5 16.2 %all-to-all-done = bf16[64,16,256]{2,1,0:T(8,128)(2,1)S(1)} async-done(((bf16[64,16,256]{2,1,0:T(8,128)(2,1)}), bf16[64,16,256]{2,1,0:T(8,128)(2,1)S(1)}, u32[]{:S(2)}, u32[]{:S(2)}) %all-to-all-start) | async-done | bytes 524320 | tf_op jit(solution)/shard_map/all_to_all | solution.py:14
  41.7 0.2 multiply_reduce_fusion
  41.9 0.1 mul.50
  42.0 1.3 fusion.2
  43.3 0.5 fusion.3
  43.8 14.0 %psum.56 = f32[256]{0:T(256)S(1)} all-reduce(f32[256]{0:T(256)S(1)} %bitcast.47), channel_id=1, replica_groups=mesh['items'=8,'codes'=64] {'items'}, use_global_device_ids=true, to_apply=%region_2.0 | all-reduce | flops 256 | bytes 2048 | tf_op jit(solution)/shard_map/psum | solution.py:45
  57.8 1.0 fusion.6
  58.8 127.3 %psum.57 = f32[1024]{0:T(1024)S(1)} all-reduce(f32[1024]{0:T(1024)S(1)} %bitcast.37), channel_id=1, replica_groups=mesh['items'=8,'codes'=64] {'codes'}, use_global_device_ids=true, to_apply=%region_3.0 | all-reduce | flops 1024 | bytes 8192 | tf_op jit(solution)/shard_map/psum | solution.py:49
  186.1 0.5 fusion.7
  186.6 11.2 %psum.58 = f32[256]{0:T(256)S(1)} all-reduce(f32[256]{0:T(256)S(1)} %bitcast.44), channel_id=1, replica_groups=mesh['items'=8,'codes'=64] {'items'}, use_global_device_ids=true, to_apply=%region_4.0 | all-reduce | flops 256 | bytes 2048 | tf_op jit(solution)/shard_map/psum | solution.py:45
  197.8 1.0 fusion.8
  198.8 127.8 %psum.59 = f32[1024]{0:T(1024)S(1)} all-reduce(f32[1024]{0:T(1024)S(1)} %bitcast.39), channel_id=1, replica_groups=mesh['items'=8,'codes'=64] {'codes'}, use_global_device_ids=true, to_apply=%region_5.0 | all-reduce | flops 1024 | bytes 8192 | tf_op jit(solution)/shard_map/psum | solution.py:49
  326.6 0.5 fusion.9
  327.1 11.6 %psum.60 = f32[256]{0:T(256)S(1)} all-reduce(f32[256]{0:T(256)S(1)} %bitcast.46), channel_id=1, replica_groups=mesh['items'=8,'codes'=64] {'items'}, use_global_device_ids=true, to_apply=%region_6.0 | all-reduce | flops 256 | bytes 2048 | tf_op jit(solution)/shard_map/psum | solution.py:45
  338.7 1.0 fusion.10
  339.7 127.8 %psum.61 = f32[1024]{0:T(1024)S(1)} all-reduce(f32[1024]{0:T(1024)S(1)} %bitcast.41), channel_id=1, replica_groups=mesh['items'=8,'codes'=64] {'codes'}, use_global_device_ids=true, to_apply=%region_7.0 | all-reduce | flops 1024 | bytes 8192 | tf_op jit(solution)/shard_map/psum | solution.py:49
  467.5 1.1 convert_reduce_fusion
  468.6 2.1 fusion.11
  470.7 0.0 all-reduce.2.cloned.1.call-update
  470.7 0.0 all-gather.2.cloned.1.call-start
  470.7 0.5 all-gather.2.cloned.1.call-update
  471.3 4.7 all-to-all-start.1
  476.0 12.6 %psum.63 = f32[256]{0:T(256)S(1)} all-reduce(f32[256]{0:T(256)S(1)} %get-tuple-element.2), channel_id=1, replica_groups=mesh['items'=8,'codes'=64] {'items'}, use_global_device_ids=true, to_apply=%region_10.0 | all-reduce | flops 256 | bytes 2048 | tf_op jit(solution)/shard_map/psum | solution.py:58
  488.6 46.5 %all-reduce.2.cloned.1.call-done = f32[256,256]{1,0:T(8,128)} async-done(((f32[256,256]{1,0:T(8,128)}), f32[256,256]{1,0:T(8,128)}) %all-reduce.2.cloned.1.call-update) | async-done | bytes 262160 | tf_op jit(solution)/shard_map/psum | solution.py:58
  535.1 1.8 broadcast_divide_fusion
  536.9 0.0 all-to-all-done.1
  536.9 18.4 %all-gather.2.cloned.1.call-done = bf16[16384,256]{1,0:T(8,128)(2,1)} async-done(((bf16[256,256]{1,0:T(8,128)(2,1)}), bf16[16384,256]{1,0:T(8,128)(2,1)}) %all-gather.2.cloned.1.call-update) | async-done | bytes 8388624 | tf_op jit(solution)/shard_map/all_gather | solution.py:63
  555.3 0.0 copy-done
  555.3 5.2 convolution_subtract_fusion
  (9 shorter events, 0.1 us)
Async XLA Ops:
  8.0 547.3 %copy-start = (bf16[16,256]{1,0:T(8,128)(2,1)S(1)}, bf16[16,256]{1,0:T(8,128)(2,1)}, u32[]{:S(2)}) copy-start(bf16[16,256]{1,0:T(8,128)(2,1)} %param.2) | copy-start | bytes 24580
  9.6 32.1 %all-to-all-start = ((bf16[64,16,256]{2,1,0:T(8,128)(2,1)}), bf16[64,16,256]{2,1,0:T(8,128)(2,1)S(1)}, u32[]{:S(2)}, u32[]{:S(2)}) async-start(bf16[64,16,256]{2,1,0:T(8,128)(2,1)} %stack.2), calls=%async_computation | async-start | bytes 1048576 | tf_op jit(solution)/shard_map/all_to_all | solution.py:14
  24.4 510.7 %all-reduce.2.cloned.1.call-start = ((), (), s32[]{:S(2)}) async-start(), calls=%async_computation.2 | async-start | bytes 524288 | tf_op jit(solution)/shard_map/psum | solution.py:58
  470.7 84.6 %all-gather.2.cloned.1.call-start = ((), (), s32[]{:S(2)}) async-start(), calls=%async_computation.3 | async-start | bytes 8519680 | tf_op jit(solution)/shard_map/all_gather | solution.py:63
  471.3 65.6 %all-to-all-start.1 = ((bf16[64,16,256]{2,1,0:T(8,128)(2,1)}), bf16[64,16,256]{2,1,0:T(8,128)(2,1)S(1)}, u32[]{:S(2)}, u32[]{:S(2)}) async-start(bf16[64,16,256]{2,1,0:T(8,128)(2,1)} %bitcast.12), calls=%async_computation.1 | async-start | bytes 1048576 | tf_op jit(solution)/shard_map/all_to_all | solution.py:60
Sparse Core Ops, SparseCore 0:
  470.8 64.2 all-reduce.1
Sparse Core Ops, SparseCore 1:
  474.5 80.7 all-gather.1
